TPU v7x, 256 devices: a whole 4x4x8 slice. The times are simulated.
256 devices in a mesh: depth: 64 (over x, y, z_hi), comp: 4 (over z_lo, core).
Axes of the slice: x: 4, y: 4, z: 8 (z_hi: 4, z_lo: 2; z = z_hi * 2 + z_lo), core: 2. Of those that a mesh axis runs over, the one named last changes fastest.
Arguments:
- density: float32 [64, 512, 256], P('depth', 'comp'), may hold values from -4 to 4
- observed: float32 [4, 512, 256], P('comp', 'depth'), may hold values from -6 to 6
- data_weight: float32 [4, 512, 256], P('comp', 'depth'), may hold values from 0.3 to 7.5
- layer_top: float32 [64], P('depth'), may hold values from 0.5 to 8
Outputs:
- density_new: float32 [64, 512, 256], P('depth', 'comp')
- weighted_error: float32 [4, 512, 256], P('comp', 'depth')
All inputs are finite; a program needn't handle non-finite values.
Results may differ from a plain program's by a relative error of at most 0.0001.
Values sent between devices are 32-bit elements; how exact they have to be, the bound alone decides.
No kernel may reach another device: no remote copies, remote signals or barrier semaphores. Data moves between devices by JAX's collectives and lax.ppermute only.
A program may use at most 64 MiB of HBM per device.

v0:
```python
import math
import jax
import jax.numpy as jnp
from jax import lax
from jax.sharding import PartitionSpec as P

ITERS = 2
TWO_PI = 2.0 * math.pi


def matmul(left, right):
    return jnp.dot(left, right, precision=lax.Precision.HIGHEST, preferred_element_type=jnp.float32)


def tables(count):
    index = lax.iota(jnp.int32, count)
    product = index[:, None] * index[None, :] % count
    angle = product.astype(jnp.float32) * (TWO_PI / count)
    return (jnp.cos(angle), jnp.sin(angle))


def wavenumbers(count):
    index = lax.iota(jnp.int32, count)
    signed = jnp.where(index < (count - 1) // 2 + 1, index, index - count)
    return signed.astype(jnp.float32) * (TWO_PI / count)


def kernel_parts(top, comp_index, rows_all, cols_all):
    kx = wavenumbers(rows_all)[:, None]
    ky = wavenumbers(cols_all)[None, :]
    kabs = jnp.sqrt(kx * kx + ky * ky)
    floor_k = jnp.maximum(kabs, TWO_PI / max(rows_all, cols_all))
    decay = 4.0 * jnp.exp(-kabs * top) * (1.0 - jnp.exp(-kabs))
    zeros = jnp.zeros_like(kabs)
    real_part = jnp.where(
        comp_index == 0,
        decay,
        jnp.where(comp_index == 3, decay * (-(kx * kx) / (floor_k * floor_k)), zeros),
    )
    imag_part = jnp.where(
        comp_index == 1,
        decay * (kx / floor_k),
        jnp.where(comp_index == 2, decay * (ky / floor_k), zeros),
    )
    return (real_part, imag_part)


def along_rows(field, cos_y, sin_y):
    return (matmul(field, cos_y), -matmul(field, sin_y))


def add_columns(part_re, part_im, cos_cols, sin_cols):
    new_re = matmul(cos_cols, part_re) + matmul(sin_cols, part_im)
    new_im = matmul(cos_cols, part_im) - matmul(sin_cols, part_re)
    return (new_re, new_im)


def inverse_rows(spec_re, spec_im, cos_rows, sin_rows, cos_y, sin_y, scale):
    mixed_re = matmul(cos_rows, spec_re) - matmul(sin_rows, spec_im)
    mixed_im = matmul(cos_rows, spec_im) + matmul(sin_rows, spec_re)
    return (matmul(mixed_re, cos_y) - matmul(mixed_im, sin_y)) * scale


def body(density, observed, data_weight, layer_top):
    own_rows = density.shape[1]
    comps = lax.axis_size("comp")
    rows_all = own_rows * comps
    cols_all = density.shape[2]
    comp_index = lax.axis_index("comp")
    cos_x, sin_x = tables(rows_all)
    cos_y, sin_y = tables(cols_all)
    scale = 1.0 / (rows_all * cols_all)
    kernels = [kernel_parts(layer_top[0], comp_index, rows_all, cols_all)]
    weight = data_weight[0]
    measured = observed[0]

    def spectrum(field):
        part_re, part_im = along_rows(field, cos_y, sin_y)
        return add_columns(part_re, part_im, cos_x, sin_x)

    def forward_once(fields):
        spec_re, spec_im = spectrum(fields[0])
        kre, kim = kernels[0]
        total_re = kre * spec_re - kim * spec_im
        total_im = kre * spec_im + kim * spec_re
        return lax.psum_scatter(
            inverse_rows(total_re, total_im, cos_x, sin_x, cos_y, sin_y, scale),
            "depth",
            scatter_dimension=0,
            tiled=True,
        )

    def forward(fields):
        return forward_once(fields)

    dens_full = lax.all_gather(density, "comp", axis=1, tiled=True)
    dens_strip = density
    predicted = forward([dens_full[0]])
    weighted_error = weight * (predicted - measured)
    for step in range(ITERS):
        weighted_res = weight * weighted_error
        add_part_re, add_part_im = along_rows(
            lax.all_gather(weighted_res, "depth", axis=0, tiled=True), cos_y, sin_y
        )
        res_re, res_im = add_columns(add_part_re, add_part_im, cos_x, sin_x)
        kre, kim = kernels[0]
        grad_re = kre * res_re + kim * res_im
        grad_im = kre * res_im - kim * res_re
        terms = [inverse_rows(grad_re, grad_im, cos_x, sin_x, cos_y, sin_y, scale)]
        data_grad = jnp.stack(terms)
        quad_strip = 1.0 / (dens_strip * dens_strip + 0.25)
        grad_strip = lax.psum_scatter(data_grad, "comp", scatter_dimension=1, tiled=True) + 0.5 * (
            quad_strip * dens_strip
        )
        grad_full = lax.all_gather(grad_strip, "comp", axis=1, tiled=True)
        grad_sq = jnp.sum(grad_strip * grad_strip)
        quad_sq = jnp.sum(quad_strip * grad_strip * grad_strip)
        grad_sq, quad_sq = lax.psum((grad_sq, quad_sq), ("depth", "comp"))
        image = forward([grad_full[0]])
        weighted_image = weight * image
        curv = jnp.sum(weighted_image * weighted_image)
        curv = lax.psum(curv, ("depth", "comp"))
        alpha = grad_sq / (curv + 0.5 * quad_sq)
        dens_strip = dens_strip - alpha * grad_strip
        predicted = predicted - alpha * image
        weighted_error = weight * (predicted - measured)
    return (dens_strip, weighted_error[None])


def solution(mesh):
    return jax.shard_map(
        body,
        mesh=mesh,
        in_specs=(
            P("depth", "comp", None),
            P("comp", "depth", None),
            P("comp", "depth", None),
            P("depth"),
        ),
        out_specs=(P("depth", "comp", None), P("comp", "depth", None)),
        check_vma=False,
    )
```

profile of v0, /device:TPU:1, one launch (start us, length us, event | category | flops | bytes accessed | tf_op | source)
XLA Modules:
  0.0 2017.7 jit_solution(2522826895115508715)
XLA Ops:
  7.3 9.8 all_gather.15
  52.4 5.7 convolution_subtract_fusion.8
  59.6 5.9 convolution_add_fusion.8
  68.0 334.6 %reduce-scatter.6.cloned.1.call-done = f32[8,256]{1,0:T(8,128)} async-done(((f32[512,256]{1,0:T(8,128)}), f32[8,256]{1,0:T(8,128)}) %reduce-scatter.6.cloned.1.call-update) | async-done | bytes 8208 | tf_op jit(solution)/shard_map/reduce_scatter | solution.py:86
  403.3 161.1 %all_gather.16 = f32[512,256]{1,0:T(8,128)S(1)} all-gather(f32[8,256]{1,0:T(8,128)S(1)} %multiply_multiply_fusion.3), channel_id=1, replica_groups=mesh['depth'=64,'comp'=4] {'depth'}, dimensions={0}, use_global_device_ids=true | all-gather | bytes 532480 | tf_op jit(solution)/shard_map/all_gather | solution.py:103
  584.5 5.8 convolution_subtract_fusion.7
  601.2 5.7 convolution_subtract_fusion.6
  608.5 5.9 convolution_add_fusion.6
  616.9 93.4 %reduce-scatter.8.cloned.1.call-done = f32[1,128,256]{2,1,0:T(8,128)} async-done(((f32[1,512,256]{2,1,0:T(8,128)}), f32[1,128,256]{2,1,0:T(8,128)}) %reduce-scatter.8.cloned.1.call-update) | async-done | bytes 131088 | tf_op jit(solution)/shard_map/reduce_scatter | solution.py:112
  711.9 7.3 all_gather.17
  739.1 5.8 convolution_subtract_fusion.5
  763.2 5.9 convolution_add_fusion.4
  771.5 333.5 %reduce-scatter.10.cloned.1.call-done = f32[8,256]{1,0:T(8,128)} async-done(((f32[512,256]{1,0:T(8,128)}), f32[8,256]{1,0:T(8,128)}) %reduce-scatter.10.cloned.1.call-update) | async-done | bytes 8208 | tf_op jit(solution)/shard_map/reduce_scatter | solution.py:86
  1106.4 123.9 %all-reduce.1 = (f32[]{:T(128)}, f32[]{:T(128)}, f32[]{:T(128)}) all-reduce(f32[]{:T(128)} %get-tuple-element.5, f32[]{:T(128)} %fusion.127, f32[]{:T(128)} %get-tuple-element.4), channel_id=1, replica_groups=mesh['depth'=64,'comp'=4] {'depth','comp'}, use_global_device_ids=true, to_apply=%region_3.4 | all-reduce | flops 3 | bytes 24 | tf_op jit(solution)/shard_map/psum | solution.py:118
  1232.1 161.9 %all_gather.18 = f32[512,256]{1,0:T(8,128)S(1)} all-gather(f32[8,256]{1,0:T(8,128)S(1)} %multiply_multiply_fusion.2), channel_id=1, replica_groups=mesh['depth'=64,'comp'=4] {'depth'}, dimensions={0}, use_global_device_ids=true | all-gather | bytes 532480 | tf_op jit(solution)/shard_map/all_gather | solution.py:103
  1414.0 5.8 convolution_subtract_fusion.3
  1430.8 5.7 convolution_subtract_fusion.2
  1438.1 5.9 convolution_add_fusion.2
  1446.4 41.4 %reduce-scatter.12.cloned.1.call-done = f32[1,128,256]{2,1,0:T(8,128)} async-done(((f32[1,512,256]{2,1,0:T(8,128)}), f32[1,128,256]{2,1,0:T(8,128)}) %reduce-scatter.12.cloned.1.call-update) | async-done | bytes 131088 | tf_op jit(solution)/shard_map/reduce_scatter | solution.py:112
  1489.4 7.3 all_gather.19
  1516.6 5.8 convolution_subtract_fusion.1
  1540.7 5.8 convolution_add_fusion
  1548.8 333.5 %reduce-scatter.14.cloned.1.call-done = f32[8,256]{1,0:T(8,128)} async-done(((f32[512,256]{1,0:T(8,128)}), f32[8,256]{1,0:T(8,128)}) %reduce-scatter.14.cloned.1.call-update) | async-done | bytes 8208 | tf_op jit(solution)/shard_map/reduce_scatter | solution.py:86
  1883.6 123.9 %all-reduce = (f32[]{:T(128)}, f32[]{:T(128)}, f32[]{:T(128)}) all-reduce(f32[]{:T(128)} %get-tuple-element.3, f32[]{:T(128)} %fusion.125, f32[]{:T(128)} %get-tuple-element.2), channel_id=1, replica_groups=mesh['depth'=64,'comp'=4] {'depth','comp'}, use_global_device_ids=true, to_apply=%region_11.12 | all-reduce | flops 3 | bytes 24 | tf_op jit(solution)/shard_map/psum | solution.py:118
  (81 shorter events, 197.4 us)
Async XLA Ops:
  7.2 395.5 %reduce-scatter.6.cloned.1.call-start = ((), (), s32[]{:S(2)}) async-start(), calls=%async_computation.5 | async-start | bytes 532480 | tf_op jit(solution)/shard_map/reduce_scatter | solution.py:86
  67.9 334.7 %copy-start.1 = (f32[1,8,256]{2,1,0:T(8,128)S(1)}, f32[1,8,256]{2,1,0:T(8,128)}, u32[]{:S(2)}) copy-start(f32[1,8,256]{2,1,0:T(8,128)} %param.6) | copy-start | bytes 24580
  67.9 334.7 %copy-start.3 = (f32[1,8,256]{2,1,0:T(8,128)S(1)}, f32[1,8,256]{2,1,0:T(8,128)}, u32[]{:S(2)}) copy-start(f32[1,8,256]{2,1,0:T(8,128)} %param.5) | copy-start | bytes 24580
  68.0 642.3 %reduce-scatter.8.cloned.1.call-start = ((), (), s32[]{:S(2)}) async-start(), calls=%async_computation.6 | async-start | bytes 655360 | tf_op jit(solution)/shard_map/reduce_scatter | solution.py:112
  616.8 93.4 %copy-start = (f32[1,128,256]{2,1,0:T(8,128)S(1)}, f32[1,128,256]{2,1,0:T(8,128)}, u32[]{:S(2)}) copy-start(f32[1,128,256]{2,1,0:T(8,128)} %param.4) | copy-start | bytes 393220
  616.8 488.1 %reduce-scatter.10.cloned.1.call-start = ((), (), s32[]{:S(2)}) async-start(), calls=%async_computation.7 | async-start | bytes 532480 | tf_op jit(solution)/shard_map/reduce_scatter | solution.py:86
  771.5 716.3 %reduce-scatter.12.cloned.1.call-start = ((), (), s32[]{:S(2)}) async-start(), calls=%async_computation.8 | async-start | bytes 655360 | tf_op jit(solution)/shard_map/reduce_scatter | solution.py:112
  1106.3 125.8 %copy-start.4 = (f32[8,256]{1,0:T(8,128)S(1)}, f32[8,256]{1,0:T(8,128)}, u32[]{:S(2)}) copy-start(f32[8,256]{1,0:T(8,128)} %reduce-scatter.6.cloned.1.call-done) | copy-start | bytes 24580
  1106.4 125.8 %copy-start.2 = (f32[8,256]{1,0:T(8,128)S(1)}, f32[8,256]{1,0:T(8,128)}, u32[]{:S(2)}) copy-start(f32[8,256]{1,0:T(8,128)} %reduce-scatter.10.cloned.1.call-done) | copy-start | bytes 24580
  1446.4 436.0 %reduce-scatter.14.cloned.1.call-start = ((), (), s32[]{:S(2)}) async-start(), calls=%async_computation.9 | async-start | bytes 532480 | tf_op jit(solution)/shard_map/reduce_scatter | solution.py:86
  2009.4 0.7 copy-start.5
Sparse Core Ops, SparseCore 0:
  68.1 334.4 reduce-scatter.5
  616.9 93.2 reduce-scatter.7
  771.6 333.3 reduce-scatter.9
  1446.5 41.2 reduce-scatter.11
  1548.9 333.3 reduce-scatter.13
where the time goes:
time: 2030 us; the launch traced here: 2020 us
  waiting for transfers between devices  1140 us (56%)
  blocking collectives  595 us (29%)
  matrix products  259 us (13%)
    reduce_scatter x3, waiting for transfers between devices, forward_once(): lax.psum_scatter(inverse_rows(total_re, total_im, cos_x, sin_x, cos_y, si...  1000 us
    all_gather x2, blocking collectives, body(): lax.all_gather(weighted_res, 'depth', axis=0, tiled=True)  323 us
    dot_general x60, matrix products, matmul(): jnp.dot(left, right, precision=lax.Precision.HIGHEST, preferred_element_t...  259 us
    psum x2, blocking collectives, body(): grad_sq, quad_sq = lax.psum((grad_sq, quad_sq), ('depth', 'comp'))  248 us
    reduce_scatter x2, waiting for transfers between devices, body(): lax.psum_scatter(data_grad, 'comp', scatter_dimension=1, tiled=True)  135 us
  transfers between devices with their start and end apart: 5, of which 5 were waited for; matrix products, arithmetic and copies ran while one was open for 0% of the time, Pallas kernels for 0%

commit v1 on v0

--- a/solution.py
+++ b/solution.py
@@ -6,6 +6,11 @@
 
 ITERS = 2
 TWO_PI = 2.0 * math.pi
+
+
+def all_by_exchange(x, mesh_axis, dim):
+    outgoing = jnp.stack([x] * lax.axis_size(mesh_axis))
+    return jnp.concatenate(lax.all_to_all(outgoing, mesh_axis, 0, 0), axis=dim)
 
 
 def matmul(left, right):
@@ -100,7 +105,7 @@
     for step in range(ITERS):
         weighted_res = weight * weighted_error
         add_part_re, add_part_im = along_rows(
-            lax.all_gather(weighted_res, "depth", axis=0, tiled=True), cos_y, sin_y
+            all_by_exchange(weighted_res, "depth", 0), cos_y, sin_y
         )
         res_re, res_im = add_columns(add_part_re, add_part_im, cos_x, sin_x)
         kre, kim = kernels[0]

time: 2030 us -> 1700 us (0.84)
  blocking collectives: 595 us -> 316 us
  waiting for transfers between devices: 1140 us -> 1090 us
    all_gather x2 -> x0, blocking collectives: 323 us -> none  [body(): lax.all_gather(weighted_res, 'depth', axis=0, tiled=True)]
    reduce_scatter x2, waiting for transfers between devices: 135 us -> 90.1 us  [body(): lax.psum_scatter(data_grad, 'comp', scatter_dimension=1, tiled=True)]
    all_to_all x0 -> x2, blocking collectives: none -> 42.9 us  [all_by_exchange(): return jnp.concatenate(lax.all_to_all(outgoing, mesh_axis, 0, 0), axis=dim)]
where the time goes in v1:
time: 1700 us
  waiting for transfers between devices  1090 us (64%)
  blocking collectives  316 us (19%)
  matrix products  259 us (15%)
  between operations  19.1 us (1%)
    reduce_scatter x3, waiting for transfers between devices, forward_once(): lax.psum_scatter(inverse_rows(total_re, total_im, cos_x, sin_x, cos_y, si...  1000 us
    dot_general x60, matrix products, matmul(): jnp.dot(left, right, precision=lax.Precision.HIGHEST, preferred_element_t...  259 us
    psum x2, blocking collectives, body(): grad_sq, quad_sq = lax.psum((grad_sq, quad_sq), ('depth', 'comp'))  248 us
    reduce_scatter x2, waiting for transfers between devices, body(): lax.psum_scatter(data_grad, 'comp', scatter_dimension=1, tiled=True)  90.1 us
    all_to_all x2, blocking collectives, all_by_exchange(): return jnp.concatenate(lax.all_to_all(outgoing, mesh_axis, 0, 0), axis=dim)  42.9 us
  transfers between devices with their start and end apart: 5, of which 5 were waited for; matrix products, arithmetic and copies ran while one was open for 0% of the time, Pallas kernels for 0%

profile of v1, /device:TPU:1, one launch (start us, length us, event | category | flops | bytes accessed | tf_op | source)
XLA Modules:
  0.0 1695.1 jit_solution(3875936726062198256)
XLA Ops:
  7.3 9.8 all_gather.9
  52.4 5.9 convolution_subtract_fusion.8
  59.8 5.7 convolution_add_fusion.8
  68.0 334.9 %reduce-scatter.6.cloned.1.call-done = f32[8,256]{1,0:T(8,128)} async-done(((f32[512,256]{1,0:T(8,128)}), f32[8,256]{1,0:T(8,128)}) %reduce-scatter.6.cloned.1.call-update) | async-done | bytes 8208 | tf_op jit(solution)/shard_map/reduce_scatter | solution.py:91
  403.6 19.6 %all_to_all.10 = f32[64,8,256]{2,1,0:T(8,128)S(1)} all-to-all(f32[64,8,256]{2,1,0:T(8,128)S(1)} %stack.8), channel_id=1, replica_groups=mesh['depth'=64,'comp'=4] {'depth'}, dimensions={0} | all-to-all | bytes 1048576 | tf_op jit(solution)/shard_map/all_to_all | solution.py:13
  443.2 6.0 convolution_subtract_fusion.7
  467.4 5.7 convolution_add_fusion.6
  475.6 71.0 %reduce-scatter.8.cloned.1.call-done = f32[1,128,256]{2,1,0:T(8,128)} async-done(((f32[1,512,256]{2,1,0:T(8,128)}), f32[1,128,256]{2,1,0:T(8,128)}) %reduce-scatter.8.cloned.1.call-update) | async-done | bytes 131088 | tf_op jit(solution)/shard_map/reduce_scatter | solution.py:117
  548.2 7.3 all_gather.10
  575.5 6.0 convolution_subtract_fusion.5
  599.8 5.9 convolution_add_fusion.4
  608.1 333.7 %reduce-scatter.10.cloned.1.call-done = f32[8,256]{1,0:T(8,128)} async-done(((f32[512,256]{1,0:T(8,128)}), f32[8,256]{1,0:T(8,128)}) %reduce-scatter.10.cloned.1.call-update) | async-done | bytes 8208 | tf_op jit(solution)/shard_map/reduce_scatter | solution.py:91
  943.2 124.5 %all-reduce.1 = (f32[]{:T(128)}, f32[]{:T(128)}, f32[]{:T(128)}) all-reduce(f32[]{:T(128)} %get-tuple-element.5, f32[]{:T(128)} %fusion.131, f32[]{:T(128)} %get-tuple-element.4), channel_id=1, replica_groups=mesh['depth'=64,'comp'=4] {'depth','comp'}, use_global_device_ids=true, to_apply=%region_3.4 | all-reduce | flops 3 | bytes 24 | tf_op jit(solution)/shard_map/psum | solution.py:123
  1069.6 23.3 %all_to_all.11 = f32[64,8,256]{2,1,0:T(8,128)S(1)} all-to-all(f32[64,8,256]{2,1,0:T(8,128)S(1)} %stack.10), channel_id=1, replica_groups=mesh['depth'=64,'comp'=4] {'depth'}, dimensions={0} | all-to-all | bytes 1048576 | tf_op jit(solution)/shard_map/all_to_all | solution.py:13
  1112.9 5.8 convolution_subtract_fusion.3
  1129.7 5.7 convolution_subtract_fusion.2
  1137.0 5.9 convolution_add_fusion.2
  1145.3 19.0 %reduce-scatter.12.cloned.1.call-done = f32[1,128,256]{2,1,0:T(8,128)} async-done(((f32[1,512,256]{2,1,0:T(8,128)}), f32[1,128,256]{2,1,0:T(8,128)}) %reduce-scatter.12.cloned.1.call-update) | async-done | bytes 131088 | tf_op jit(solution)/shard_map/reduce_scatter | solution.py:117
  1166.0 7.3 all_gather.11
  1193.2 5.8 convolution_subtract_fusion.1
  1210.0 5.7 convolution_subtract_fusion
  1217.3 5.8 convolution_add_fusion
  1225.4 334.2 %reduce-scatter.14.cloned.1.call-done = f32[8,256]{1,0:T(8,128)} async-done(((f32[512,256]{1,0:T(8,128)}), f32[8,256]{1,0:T(8,128)}) %reduce-scatter.14.cloned.1.call-update) | async-done | bytes 8208 | tf_op jit(solution)/shard_map/reduce_scatter | solution.py:91
  1560.9 124.0 %all-reduce = (f32[]{:T(128)}, f32[]{:T(128)}, f32[]{:T(128)}) all-reduce(f32[]{:T(128)} %get-tuple-element.3, f32[]{:T(128)} %fusion.129, f32[]{:T(128)} %get-tuple-element.2), channel_id=1, replica_groups=mesh['depth'=64,'comp'=4] {'depth','comp'}, use_global_device_ids=true, to_apply=%region_11.12 | all-reduce | flops 3 | bytes 24 | tf_op jit(solution)/shard_map/psum | solution.py:123
  (83 shorter events, 197.4 us)
Async XLA Ops:
  7.2 395.7 %reduce-scatter.6.cloned.1.call-start = ((), (), s32[]{:S(2)}) async-start(), calls=%async_computation.7 | async-start | bytes 532480 | tf_op jit(solution)/shard_map/reduce_scatter | solution.py:91
  67.9 334.9 %copy-start.1 = (f32[1,8,256]{2,1,0:T(8,128)S(1)}, f32[1,8,256]{2,1,0:T(8,128)}, u32[]{:S(2)}) copy-start(f32[1,8,256]{2,1,0:T(8,128)} %param.6) | copy-start | bytes 24580
  67.9 334.9 %copy-start.3 = (f32[1,8,256]{2,1,0:T(8,128)S(1)}, f32[1,8,256]{2,1,0:T(8,128)}, u32[]{:S(2)}) copy-start(f32[1,8,256]{2,1,0:T(8,128)} %param.5) | copy-start | bytes 24580
  67.9 478.7 %reduce-scatter.8.cloned.1.call-start = ((), (), s32[]{:S(2)}) async-start(), calls=%async_computation.8 | async-start | bytes 655360 | tf_op jit(solution)/shard_map/reduce_scatter | solution.py:117
  475.5 71.1 %copy-start = (f32[1,128,256]{2,1,0:T(8,128)S(1)}, f32[1,128,256]{2,1,0:T(8,128)}, u32[]{:S(2)}) copy-start(f32[1,128,256]{2,1,0:T(8,128)} %param.4) | copy-start | bytes 393220
  475.5 466.3 %reduce-scatter.10.cloned.1.call-start = ((), (), s32[]{:S(2)}) async-start(), calls=%async_computation.9 | async-start | bytes 532480 | tf_op jit(solution)/shard_map/reduce_scatter | solution.py:91
  608.1 556.3 %reduce-scatter.12.cloned.1.call-start = ((), (), s32[]{:S(2)}) async-start(), calls=%async_computation.10 | async-start | bytes 655360 | tf_op jit(solution)/shard_map/reduce_scatter | solution.py:117
  943.2 126.3 %copy-start.4 = (f32[8,256]{1,0:T(8,128)S(1)}, f32[8,256]{1,0:T(8,128)}, u32[]{:S(2)}) copy-start(f32[8,256]{1,0:T(8,128)} %reduce-scatter.6.cloned.1.call-done) | copy-start | bytes 24580
  943.2 126.3 %copy-start.2 = (f32[8,256]{1,0:T(8,128)S(1)}, f32[8,256]{1,0:T(8,128)}, u32[]{:S(2)}) copy-start(f32[8,256]{1,0:T(8,128)} %reduce-scatter.10.cloned.1.call-done) | copy-start | bytes 24580
  1145.3 414.3 %reduce-scatter.14.cloned.1.call-start = ((), (), s32[]{:S(2)}) async-start(), calls=%async_computation.11 | async-start | bytes 532480 | tf_op jit(solution)/shard_map/reduce_scatter | solution.py:91
  1686.8 0.7 copy-start.5
Sparse Core Ops, SparseCore 0:
  68.0 334.7 reduce-scatter.5
  475.7 70.9 reduce-scatter.7
  608.2 333.5 reduce-scatter.9
  1145.4 18.9 reduce-scatter.11
  1225.6 334.0 reduce-scatter.13
